TPU v7x, 256 devices: a whole 4x4x8 slice. The times are simulated.
256 devices in a mesh: loop: 16 (over z, x_lo), row: 4 (over x_hi, core), col: 4 (over y).
Axes of the slice: x: 4 (x_hi: 2, x_lo: 2; x = x_hi * 2 + x_lo), y: 4, z: 8, core: 2. Of those that a mesh axis runs over, the one named last changes fastest.
Arguments:
- interval_blocks: bfloat16 [16, 4, 2048, 2048], P('loop', None, 'row', 'col'), may hold values from -0.15625 to 0.15625
- interval_pivots: int32 [16, 3, 2048], P('loop'), may hold values from 0 to 2047, each once within a row
- boundary_pivots: int32 [16, 2048], replicated, may hold values from 0 to 2047, each once within a row
- interval_residuals: bfloat16 [16, 4, 2048], P('loop', None, ('row', 'col')), may hold values from -0.23925781 to 0.23925781
Outputs:
- reduced_block: bfloat16 [16, 2048, 2048], P('loop', 'row', 'col')
- reduced_rhs: float32 [16, 2048], P('loop', ('row', 'col'))
Inputs may be any that keep to these rules, and one draw needn't show every extreme that they name: Each row of interval_pivots is a permutation of 0 to 2047. Each row of boundary_pivots is a permutation of 0 to 2047.
All inputs are finite; a program needn't handle non-finite values.
Results may differ from a plain program's by a relative error of at most 0.018.
Values may be sent and summed in bfloat16 or wider, within the bound.
A program may use at most 64 MiB of HBM per device.

v0:
```python
import jax
import jax.numpy as jnp
from jax import lax
from jax.sharding import PartitionSpec as P


def from_behind(value, axis, by):
    devices = lax.axis_size(axis)
    return lax.ppermute(value, axis, [(i, (i + by) % devices) for i in range(devices)])


def compose(left_block, right_block, right_vector, pivots, added):
    column_panel = lax.all_gather(right_block, "row", axis=0, tiled=True)
    full_vector = lax.all_gather(right_vector, ("row", "col"), axis=0, tiled=True)
    permuted = jnp.take(column_panel, pivots, axis=0)
    moved = jnp.take(full_vector, pivots, axis=0)
    segment = lax.all_gather(left_block, "col", axis=1, tiled=True)
    product = jnp.dot(segment, permuted, preferred_element_type=jnp.float32)
    applied = jnp.dot(segment, moved, preferred_element_type=jnp.float32)
    share_size = added.shape[0]
    own_part = lax.dynamic_slice_in_dim(applied, lax.axis_index("col") * share_size, share_size, 0)
    return (product, own_part + added.astype(jnp.float32))


def shards(interval_blocks, interval_pivots, boundary_pivots, interval_residuals):
    blocks = interval_blocks[0]
    pivot_rows = interval_pivots[0]
    residuals = interval_residuals[0]
    matrix = blocks[0]
    vector = residuals[0]
    for interval in range(1, blocks.shape[0]):
        product, applied = compose(
            blocks[interval], matrix, vector, pivot_rows[interval - 1], residuals[interval]
        )
        matrix = product.astype(jnp.bfloat16)
        vector = applied.astype(jnp.bfloat16)
    position = lax.axis_index("loop")
    count_loop = lax.axis_size("loop")
    own_pivots = lax.dynamic_index_in_dim(boundary_pivots, position, 0, keepdims=False)
    back_pivots = lax.dynamic_index_in_dim(
        boundary_pivots, (position + count_loop - 1) % count_loop, 0, keepdims=False
    )
    earlier, earlier_vector = from_behind((matrix, vector), "loop", 1)
    product, applied = compose(matrix, earlier, earlier_vector, own_pivots, vector)
    halved = product.astype(jnp.bfloat16)
    halved_vector = applied.astype(jnp.bfloat16)
    distant, distant_vector = from_behind((halved, halved_vector), "loop", 2)
    reduced, reduced_vector = compose(halved, distant, distant_vector, back_pivots, halved_vector)
    return (reduced.astype(jnp.bfloat16)[None], reduced_vector[None])


def solution(mesh):
    placed = (
        P("loop", None, "row", "col"),
        P("loop", None, None),
        P(),
        P("loop", None, ("row", "col")),
    )
    return jax.shard_map(
        shards,
        mesh=mesh,
        in_specs=placed,
        out_specs=(P("loop", "row", "col"), P("loop", ("row", "col"))),
        check_vma=False,
    )
```

profile of v0, /device:TPU:8, one launch (start us, length us, event | category | flops | bytes accessed | tf_op | source)
XLA Modules:
  0.0 394.3 jit_solution(15672747446238209155)
XLA Ops:
  7.2 0.0 all-gather.32.cloned.1.call-start
  7.2 2.9 fusion.83
  10.1 0.0 all-gather.34.cloned.1.call-start
  10.2 0.7 all-gather.34.cloned.1.call-update
  10.9 0.0 all-gather.20.cloned.1.call-start
  10.9 34.3 %all-gather.4 = bf16[1,1,2048]{2,1,0:T(2,128)(2,1)S(1)} all-gather(bf16[1,1,128]{2,1,0:T(2,128)(2,1)S(1)} %slice.51), channel_id=6, replica_groups=mesh['loop'=16,'row'=4,'col'=4] {'row','col'}, dimensions={2}, use_global_device_ids=true | all-gather | bytes 4352 | tf_op jit(solution)/shard_map/all_gather | solution.py:14
  45.3 13.1 %gather_fusion.5 = bf16[2048]{0:T(1024)(128)(2,1)S(1)} fusion(bf16[2048]{0:T(1024)(128)(2,1)S(1)} %reduce, s32[2048]{0:T(1024)S(1)} %fusion.68), kind=kCustom, calls=%fused_computation.1.clone | custom fusion | bytes 16384 | tf_op jit(solution)/shard_map/jit(_take)/gather | solution.py:16
  58.4 0.0 all-gather.32.cloned.1.call-done
  58.5 9.5 %gather_fusion = bf16[2048,512]{1,0:T(8,128)(2,1)S(1)} fusion(bf16[2048,512]{1,0:T(8,128)(2,1)} %bitcast.80, s32[2048]{0:T(1024)S(1)} %fusion.68), kind=kCustom, calls=%fused_computation.clone | custom fusion | bytes 4202496 | tf_op jit(solution)/shard_map/jit(_take)/gather | solution.py:15
  67.9 8.3 %all-gather.34.cloned.1.call-done = bf16[1,1,512,2048]{3,2,1,0:T(8,128)(2,1)} async-done(((bf16[1,1,512,512]{3,2,1,0:T(8,128)(2,1)}), bf16[1,1,512,2048]{3,2,1,0:T(8,128)(2,1)}) %all-gather.34.cloned.1.call-update) | async-done | bytes 2097168 | tf_op jit(solution)/shard_map/all_gather | solution.py:17
  76.3 4.1 %fusion.55 = bf16[512,512]{0,1:T(8,128)(2,1)} fusion(bf16[1,1,512,2048]{3,2,1,0:T(8,128)(2,1)} %all-gather.34.cloned.1.call-done, bf16[2048,512]{1,0:T(8,128)(2,1)S(1)} %gather_fusion, pred[2048]{0:T(1024)(128)(4,1)S(1)} %get-tuple-element.13), kind=kOutput, calls=%fused_computation.41 | convolution fusion | flops 1075052544 | bytes 4720640 | tf_op jit(solution)/shard_map/dot_general | solution.py:18
  80.3 0.0 all-gather.36.cloned.1.call-start
  80.4 0.5 all-gather.36.cloned.1.call-update
  80.9 0.0 all-gather.22.cloned.1.call-start
  81.0 2.2 fusion.8
  83.2 0.1 fusion.77
  83.3 33.7 %all-gather.5 = bf16[16,1,128]{2,1,0:T(2,128)(2,1)S(1)} all-gather(bf16[1,1,128]{2,1,0:T(2,128)(2,1)S(1)} %fusion.77), channel_id=1, replica_groups=mesh['loop'=16,'row'=4,'col'=4] {'row','col'}, dimensions={0}, use_global_device_ids=true | all-gather | bytes 4352 | tf_op jit(solution)/shard_map/all_gather | solution.py:14
  117.0 13.1 %gather_fusion.6 = bf16[2048]{0:T(1024)(128)(2,1)S(1)} fusion(bf16[2048]{0:T(1024)(128)(2,1)S(1)} %bitcast.77, s32[2048]{0:T(1024)S(1)} %fusion.69), kind=kCustom, calls=%fused_computation.6.clone | custom fusion | bytes 16384 | tf_op jit(solution)/shard_map/jit(_take)/gather | solution.py:16
  130.1 0.0 all-gather.20.cloned.1.call-done
  130.1 2.9 copy.8
  133.0 9.2 %gather_fusion.1 = bf16[2048,512]{1,0:T(8,128)(2,1)} fusion(bf16[2048,512]{1,0:T(8,128)(2,1)S(1)} %copy.8, s32[2048]{0:T(1024)S(1)} %fusion.69), kind=kCustom, calls=%fused_computation.2.clone | custom fusion | bytes 4202496 | tf_op jit(solution)/shard_map/jit(_take)/gather | solution.py:15
  142.2 2.1 all-gather.36.cloned.1.call-done
  144.3 4.8 %fusion.50 = bf16[512,512]{0,1:T(8,128)(2,1)} fusion(bf16[1,1,512,2048]{3,2,1,0:T(8,128)(2,1)} %all-gather.36.cloned.1.call-done, bf16[2048,512]{1,0:T(8,128)(2,1)} %gather_fusion.1, pred[2048]{0:T(1024)(128)(4,1)S(1)} %get-tuple-element.11), kind=kOutput, calls=%fused_computation.40 | convolution fusion | flops 1075052544 | bytes 4720640 | tf_op jit(solution)/shard_map/dot_general | solution.py:18
  149.1 0.0 all-gather.38.cloned.1.call-start
  149.2 0.5 all-gather.38.cloned.1.call-update
  149.7 0.0 all-gather.26.cloned.1.call-start
  149.8 0.6 fusion.4
  150.4 0.1 fusion.75
  150.5 33.7 %all-gather.6 = bf16[16,1,128]{2,1,0:T(2,128)(2,1)S(1)} all-gather(bf16[1,1,128]{2,1,0:T(2,128)(2,1)S(1)} %fusion.75), channel_id=1, replica_groups=mesh['loop'=16,'row'=4,'col'=4] {'row','col'}, dimensions={0}, use_global_device_ids=true | all-gather | bytes 4352 | tf_op jit(solution)/shard_map/all_gather | solution.py:14
  184.2 13.1 %gather_fusion.7 = bf16[2048]{0:T(1024)(128)(2,1)S(1)} fusion(bf16[2048]{0:T(1024)(128)(2,1)S(1)} %bitcast.78, s32[2048]{0:T(1024)S(1)} %fusion.70), kind=kCustom, calls=%fused_computation.7.clone | custom fusion | bytes 16384 | tf_op jit(solution)/shard_map/jit(_take)/gather | solution.py:16
  197.4 2.9 copy.9
  200.2 9.2 %gather_fusion.2 = bf16[2048,512]{1,0:T(8,128)(2,1)} fusion(bf16[2048,512]{1,0:T(8,128)(2,1)S(1)} %copy.9, s32[2048]{0:T(1024)S(1)} %fusion.70), kind=kCustom, calls=%fused_computation.3.clone | custom fusion | bytes 4202496 | tf_op jit(solution)/shard_map/jit(_take)/gather | solution.py:15
  209.4 3.7 all-gather.38.cloned.1.call-done
  213.1 4.0 %fusion.45 = bf16[512,512]{0,1:T(8,128)(2,1)S(1)} fusion(bf16[1,1,512,2048]{3,2,1,0:T(8,128)(2,1)} %all-gather.38.cloned.1.call-done, bf16[2048,512]{1,0:T(8,128)(2,1)} %gather_fusion.2, pred[2048]{0:T(1024)(128)(4,1)S(1)} %get-tuple-element.9), kind=kOutput, calls=%fused_computation.39 | convolution fusion | flops 1075052544 | bytes 4720640 | tf_op jit(solution)/shard_map/dot_general | solution.py:18
  217.1 1.5 collective-permute-start
  218.7 14.7 %collective-permute-done = bf16[512,512]{0,1:T(8,128)(2,1)S(1)} collective-permute-done((bf16[512,512]{0,1:T(8,128)(2,1)S(1)}, bf16[512,512]{0,1:T(8,128)(2,1)S(1)}, u32[]{:S(2)}, u32[]{:S(2)}) %collective-permute-start) | collective-permute-done | bytes 524320 | tf_op jit(solution)/shard_map/ppermute | solution.py:9
  233.4 0.8 copy-done.4
  234.2 0.0 all-gather.24.cloned.1.call-start
  234.3 0.7 all-gather.24.cloned.1.call-update
  235.0 0.0 all-gather.28.cloned.1.call-start
  235.0 0.9 constant_dynamic-slice_fusion
  235.9 0.6 fusion
  236.6 0.1 fusion.73
  236.7 0.2 collective-permute-start.2
  236.9 5.6 %collective-permute-done.2 = bf16[128]{0:T(256)(128)(2,1)S(1)} collective-permute-done((bf16[128]{0:T(256)(128)(2,1)S(1)}, bf16[128]{0:T(256)(128)(2,1)S(1)}, u32[]{:S(2)}, u32[]{:S(2)}) %collective-permute-start.2) | collective-permute-done | bytes 288 | tf_op jit(solution)/shard_map/ppermute | solution.py:9
  242.5 33.6 %all-gather.7 = bf16[16,1,128]{2,1,0:T(2,128)(2,1)S(1)} all-gather(bf16[1,1,128]{2,1,0:T(2,128)(2,1)S(1)} %bitcast.97), channel_id=1, replica_groups=mesh['loop'=16,'row'=4,'col'=4] {'row','col'}, dimensions={0}, use_global_device_ids=true | all-gather | bytes 4352 | tf_op jit(solution)/shard_map/all_gather | solution.py:14
  276.2 13.1 %gather_fusion.8 = bf16[2048]{0:T(1024)(128)(2,1)S(1)} fusion(bf16[2048]{0:T(1024)(128)(2,1)S(1)} %bitcast.79, s32[2048]{0:T(1024)S(1)} %fusion.71), kind=kCustom, calls=%fused_computation.8.clone | custom fusion | bytes 16384 | tf_op jit(solution)/shard_map/jit(_take)/gather | solution.py:16
  289.3 2.9 copy.10
  292.2 9.2 %gather_fusion.3 = bf16[2048,512]{1,0:T(8,128)(2,1)} fusion(bf16[2048,512]{1,0:T(8,128)(2,1)S(1)} %copy.10, s32[2048]{0:T(1024)S(1)} %fusion.71), kind=kCustom, calls=%fused_computation.4.clone | custom fusion | bytes 4202496 | tf_op jit(solution)/shard_map/jit(_take)/gather | solution.py:15
  301.4 4.5 %fusion.24 = bf16[512,512]{1,0:T(8,128)(2,1)} fusion(bf16[512,2048]{0,1:T(8,128)(2,1)} %all-gather.24.cloned.1.call-done, bf16[2048,512]{1,0:T(8,128)(2,1)} %gather_fusion.3, pred[2048]{0:T(1024)(128)(4,1)S(1)} %get-tuple-element.7), kind=kOutput, calls=%fused_computation.34 | convolution fusion | flops 1075052544 | bytes 4720640 | tf_op jit(solution)/shard_map/dot_general | solution.py:18
  305.9 0.0 all-gather.30.cloned.1.call-start
  306.0 0.1 collective-permute-start.1
  306.1 12.5 %collective-permute-done.1 = bf16[512,512]{1,0:T(8,128)(2,1)S(1)} collective-permute-done((bf16[512,512]{1,0:T(8,128)(2,1)}, bf16[512,512]{1,0:T(8,128)(2,1)S(1)}, u32[]{:S(2)}, u32[]{:S(2)}) %collective-permute-start.1) | collective-permute-done | bytes 524320 | tf_op jit(solution)/shard_map/ppermute | solution.py:9
  318.6 0.8 copy-done.5
  319.4 0.4 fusion.85
  319.8 0.1 add_convert_fusion
  319.9 0.0 collective-permute-start.3
  319.9 4.7 %collective-permute-done.3 = bf16[128]{0:T(256)(128)(2,1)S(1)} collective-permute-done((bf16[128]{0:T(256)(128)(2,1)S(1)}, bf16[128]{0:T(256)(128)(2,1)S(1)}, u32[]{:S(2)}, u32[]{:S(2)}) %collective-permute-start.3) | collective-permute-done | bytes 288 | tf_op jit(solution)/shard_map/ppermute | solution.py:9
  324.7 33.6 %all-gather.8 = bf16[16,1,128]{2,1,0:T(2,128)(2,1)S(1)} all-gather(bf16[1,1,128]{2,1,0:T(2,128)(2,1)S(1)} %bitcast.96), channel_id=1, replica_groups=mesh['loop'=16,'row'=4,'col'=4] {'row','col'}, dimensions={0}, use_global_device_ids=true | all-gather | bytes 4352 | tf_op jit(solution)/shard_map/all_gather | solution.py:14
  358.3 13.1 %gather_fusion.9 = bf16[2048]{0:T(1024)(128)(2,1)S(1)} fusion(bf16[2048]{0:T(1024)(128)(2,1)S(1)} %bitcast.76, s32[2048]{0:T(1024)S(1)} %fusion.72), kind=kCustom, calls=%fused_computation.9.clone | custom fusion | bytes 16384 | tf_op jit(solution)/shard_map/jit(_take)/gather | solution.py:16
  371.5 2.2 fusion.86
  373.7 0.6 add_bitcast_fusion
  374.3 9.4 %gather_fusion.4 = bf16[2048,512]{1,0:T(8,128)(2,1)S(1)} fusion(bf16[2048,512]{1,0:T(8,128)(2,1)} %all-gather.30.cloned.1.call-done, s32[2048]{0:T(1024)S(1)} %fusion.72), kind=kCustom, calls=%fused_computation.5.clone | custom fusion | bytes 4202496 | tf_op jit(solution)/shard_map/jit(_take)/gather | solution.py:15
  383.8 3.7 fusion.60
  (47 shorter events, 0.5 us)
Async XLA Ops:
  7.2 3.7 copy-start.7
  7.2 38.1 %copy-start.6 = (s32[1,3,2048]{2,0,1:T(1,128)S(1)}, s32[1,3,2048]{2,0,1:T(1,128)}, u32[]{:S(2)}) copy-start(s32[1,3,2048]{2,0,1:T(1,128)} %param.9) | copy-start | bytes 73732
  7.2 51.3 %all-gather.32.cloned.1.call-start = ((), (), s32[]{:S(2)}) async-start(), calls=%async_computation.6 | async-start | bytes 2621440 | tf_op jit(solution)/shard_map/all_gather | solution.py:13
  10.1 66.1 %all-gather.34.cloned.1.call-start = ((), (), s32[]{:S(2)}) async-start(), calls=%async_computation.7 | async-start | bytes 2621440 | tf_op jit(solution)/shard_map/all_gather | solution.py:17
  10.9 119.3 %all-gather.20.cloned.1.call-start = ((), (), s32[]{:S(2)}) async-start(), calls=%async_computation | async-start | bytes 2621440 | tf_op jit(solution)/shard_map/all_gather | solution.py:13
  80.3 63.9 %all-gather.36.cloned.1.call-start = ((), (), s32[]{:S(2)}) async-start(), calls=%async_computation.8 | async-start | bytes 2621440 | tf_op jit(solution)/shard_map/all_gather | solution.py:17
  80.9 116.4 %all-gather.22.cloned.1.call-start = ((), (), s32[]{:S(2)}) async-start(), calls=%async_computation.1 | async-start | bytes 2621440 | tf_op jit(solution)/shard_map/all_gather | solution.py:13
  144.3 5.5 %copy-start.2 = (bf16[1,1,512,2048]{3,2,1,0:T(8,128)(2,1)S(1)}, bf16[1,1,512,2048]{3,2,1,0:T(8,128)(2,1)}, u32[]{:S(2)}) copy-start(bf16[1,1,512,2048]{3,2,1,0:T(8,128)(2,1)} %all-gather.36.cloned.1.call-done) | copy-start | bytes 6291460
  149.1 63.9 %all-gather.38.cloned.1.call-start = ((), (), s32[]{:S(2)}) async-start(), calls=%async_computation.9 | async-start | bytes 2621440 | tf_op jit(solution)/shard_map/all_gather | solution.py:17
  149.7 139.6 %all-gather.26.cloned.1.call-start = ((), (), s32[]{:S(2)}) async-start(), calls=%async_computation.3 | async-start | bytes 2621440 | tf_op jit(solution)/shard_map/all_gather | solution.py:13
  213.1 22.8 %copy-start.1 = (bf16[1,1,512,2048]{3,2,1,0:T(8,128)(2,1)S(1)}, bf16[1,1,512,2048]{3,2,1,0:T(8,128)(2,1)}, u32[]{:S(2)}) copy-start(bf16[1,1,512,2048]{3,2,1,0:T(8,128)(2,1)} %all-gather.38.cloned.1.call-done) | copy-start | bytes 6291460
  217.1 17.1 %copy-start.3 = (bf16[512,512]{0,1:T(8,128)(2,1)}, bf16[512,512]{0,1:T(8,128)(2,1)S(1)}, u32[]{:S(2)}) copy-start(bf16[512,512]{0,1:T(8,128)(2,1)S(1)} %fusion.45) | copy-start | bytes 1572868
  217.1 16.2 %collective-permute-start = (bf16[512,512]{0,1:T(8,128)(2,1)S(1)}, bf16[512,512]{0,1:T(8,128)(2,1)S(1)}, u32[]{:S(2)}, u32[]{:S(2)}) collective-permute-start(bf16[512,512]{0,1:T(8,128)(2,1)S(1)} %fusion.45), channel_id=1, source_target_pairs={{0,16},{16,32},{32,48},{48,64},{64,80},{80,96},{96,112},{112,128},... | collective-permute-start | bytes 1572872 | tf_op jit(solution)/shard_map/ppermute | solution.py:9
  233.4 0.8 copy-start.4
  234.2 67.2 %all-gather.24.cloned.1.call-start = ((), (), s32[]{:S(2)}) async-start(), calls=%async_computation.2 | async-start | bytes 2621440 | tf_op jit(solution)/shard_map/all_gather | solution.py:17
  235.0 136.5 %all-gather.28.cloned.1.call-start = ((), (), s32[]{:S(2)}) async-start(), calls=%async_computation.4 | async-start | bytes 2621440 | tf_op jit(solution)/shard_map/all_gather | solution.py:17
  236.7 5.8 %collective-permute-start.2 = (bf16[128]{0:T(256)(128)(2,1)S(1)}, bf16[128]{0:T(256)(128)(2,1)S(1)}, u32[]{:S(2)}, u32[]{:S(2)}) collective-permute-start(bf16[128]{0:T(256)(128)(2,1)S(1)} %fusion.73), channel_id=1, source_target_pairs={{0,16},{16,32},{32,48},{48,64},{64,80},{80,96},{96,112},{112,128},... | collective-permute-start | bytes 776 | tf_op jit(solution)/shard_map/ppermute | solution.py:9
  301.4 18.0 %copy-start = (bf16[512,2048]{0,1:T(8,128)(2,1)S(1)}, bf16[512,2048]{0,1:T(8,128)(2,1)}, u32[]{:S(2)}) copy-start(bf16[512,2048]{0,1:T(8,128)(2,1)} %all-gather.24.cloned.1.call-done) | copy-start | bytes 6291460
  305.9 68.4 %all-gather.30.cloned.1.call-start = ((), (), s32[]{:S(2)}) async-start(), calls=%async_computation.5 | async-start | bytes 2621440 | tf_op jit(solution)/shard_map/all_gather | solution.py:13
  306.0 12.6 %collective-permute-start.1 = (bf16[512,512]{1,0:T(8,128)(2,1)}, bf16[512,512]{1,0:T(8,128)(2,1)S(1)}, u32[]{:S(2)}, u32[]{:S(2)}) collective-permute-start(bf16[512,512]{1,0:T(8,128)(2,1)} %fusion.24), channel_id=1, source_target_pairs={{0,32},{16,48},{32,64},{48,80},{64,96},{80,112},{96,128},{112,144}... | collective-permute-start | bytes 1572872 | tf_op jit(solution)/shard_map/ppermute | solution.py:9
  318.6 0.8 copy-start.5
  319.9 4.8 %collective-permute-start.3 = (bf16[128]{0:T(256)(128)(2,1)S(1)}, bf16[128]{0:T(256)(128)(2,1)S(1)}, u32[]{:S(2)}, u32[]{:S(2)}) collective-permute-start(bf16[128]{0:T(256)(128)(2,1)S(1)} %add_convert_fusion), channel_id=1, source_target_pairs={{0,32},{16,48},{32,64},{48,80},{64,96},{80,112},{96,128},{112,144}... | collective-permute-start | bytes 776 | tf_op jit(solution)/shard_map/ppermute | solution.py:9
Sparse Core Ops, SparseCore 0:
  10.4 32.0 all-gather.31
  44.3 31.9 all-gather.33
  80.5 30.1 all-gather.19
  112.3 31.9 all-gather.35
  149.3 30.1 all-gather.21
  181.1 31.9 all-gather.37
  234.3 29.7 all-gather.25
  266.5 31.9 all-gather.23
  306.0 31.8 all-gather.27
  339.6 30.1 all-gather.29
where the time goes:
time: 395 us; the launch traced here: 394 us
  blocking collectives  169 us (43%)
  local copies, waits for them, and re-layouts  126 us (32%)
  waiting for transfers between devices  54.3 us (14%)
  matrix products  27.2 us (7%)
  between operations  14.6 us (4%)
    all_gather x5, blocking collectives, compose(): lax.all_gather(right_vector, ('row', 'col'), axis=0, tiled=True)  169 us
    gather x5, local copies, waits for them, and re-layouts, compose(): moved = jnp.take(full_vector, pivots, axis=0)  65.4 us
    gather x5, local copies, waits for them, and re-layouts, compose(): permuted = jnp.take(column_panel, pivots, axis=0)  46.4 us
    ppermute x4, waiting for transfers between devices, from_behind(): lax.ppermute(value, axis, [(i, (i + by) % devices) for i in range(devices)])  37.5 us
    dot_general x5, matrix products, compose(): product = jnp.dot(segment, permuted, preferred_element_type=jnp.float32)  21.1 us
    all_gather x5, waiting for transfers between devices, compose(): segment = lax.all_gather(left_block, 'col', axis=1, tiled=True)  14.1 us
    all_gather x3, local copies, waits for them, and re-layouts, compose(): column_panel = lax.all_gather(right_block, 'row', axis=0, tiled=True)  8.65 us
  transfers between devices with their start and end apart: 14, of which 7 were waited for; matrix products, arithmetic and copies ran while one was open for 30% of the time, Pallas kernels for 0%

commit v1 on v0

--- a/solution.py
+++ b/solution.py
@@ -2,6 +2,19 @@
 import jax.numpy as jnp
 from jax import lax
 from jax.sharding import PartitionSpec as P
+
+
+def collect(x, axis, dim):
+    ways = lax.axis_size(axis)
+    up = [(d, (d + 1) % ways) for d in range(ways)]
+    down = [(d, (d - 1) % ways) for d in range(ways)]
+    earlier, later = ([x], [x])
+    for _ in range(ways // 2):
+        earlier.append(lax.ppermute(earlier[-1], axis, up))
+    for _ in range((ways - 1) // 2):
+        later.append(lax.ppermute(later[-1], axis, down))
+    line = jnp.concatenate([*earlier[::-1], *later[1:]], axis=dim)
+    return jnp.roll(line, (lax.axis_index(axis) - ways // 2) * x.shape[dim], axis=dim)
 
 
 def from_behind(value, axis, by):
@@ -14,7 +27,7 @@
     full_vector = lax.all_gather(right_vector, ("row", "col"), axis=0, tiled=True)
     permuted = jnp.take(column_panel, pivots, axis=0)
     moved = jnp.take(full_vector, pivots, axis=0)
-    segment = lax.all_gather(left_block, "col", axis=1, tiled=True)
+    segment = collect(left_block, "col", 1)
     product = jnp.dot(segment, permuted, preferred_element_type=jnp.float32)
     applied = jnp.dot(segment, moved, preferred_element_type=jnp.float32)
     share_size = added.shape[0]

time: 395 us -> 509 us (1.29); the launches traced: 394 us -> 501 us
  other arithmetic: 1.19 us -> 52.4 us
  starting transfers between devices: 2.26 us -> 31.7 us
  waiting for transfers between devices: 54.3 us -> 76.7 us
  matrix products: 27.2 us -> 21.4 us
    concatenate x0 -> x5, other arithmetic: none -> 51.3 us  [collect(): jnp.roll(line, (lax.axis_index(axis) - ways // 2) * x.shape[dim], axis=dim)]
    ppermute x0 -> x15, waiting for transfers between devices: none -> 40.9 us  [the longest x10 40.9 us: collect(): earlier.append(lax.ppermute(earlier[-1], axis, up))]
    ppermute x0 -> x15, starting transfers between devices: none -> 30.6 us  [the longest x10 23.7 us: collect(): earlier.append(lax.ppermute(earlier[-1], axis, up))]
    all_gather x5 -> x0, waiting for transfers between devices: 14.1 us -> none  [compose(): segment = lax.all_gather(left_block, 'col', axis=1, tiled=True)]
    gather x5, local copies, waits for them, and re-layouts: 46.4 us -> 51.8 us  [compose(): permuted = jnp.take(column_panel, pivots, axis=0)]
    all_gather x5, blocking collectives: 169 us -> 174 us  [compose(): lax.all_gather(right_vector, ('row', 'col'), axis=0, tiled=True)]
  transfers between devices with their start and end apart: 14 -> 24, of which waited for: 7 -> 9; matrix products, arithmetic and copies ran while one was open for 30% -> 24% of each run, Pallas kernels for 0% -> 0%
where the time goes in v1:
time: 509 us; the launch traced here: 501 us
  blocking collectives  174 us (34%)
  local copies, waits for them, and re-layouts  130 us (26%)
  waiting for transfers between devices  76.7 us (15%)
  other arithmetic  52.4 us (10%)
  starting transfers between devices  31.7 us (6%)
  matrix products  21.4 us (4%)
  between operations  14.4 us (3%)
    all_gather x5, blocking collectives, compose(): lax.all_gather(right_vector, ('row', 'col'), axis=0, tiled=True)  174 us
    gather x5, local copies, waits for them, and re-layouts, compose(): moved = jnp.take(full_vector, pivots, axis=0)  65.4 us
    gather x5, local copies, waits for them, and re-layouts, compose(): permuted = jnp.take(column_panel, pivots, axis=0)  51.8 us
    concatenate x5, other arithmetic, collect(): jnp.roll(line, (lax.axis_index(axis) - ways // 2) * x.shape[dim], axis=dim)  51.3 us
    ppermute x10, waiting for transfers between devices, collect(): earlier.append(lax.ppermute(earlier[-1], axis, up))  40.9 us
    ppermute x4, waiting for transfers between devices, from_behind(): lax.ppermute(value, axis, [(i, (i + by) % devices) for i in range(devices)])  35.7 us
    ppermute x10, starting transfers between devices, collect(): earlier.append(lax.ppermute(earlier[-1], axis, up))  23.7 us
    dot_general x5, matrix products, compose(): product = jnp.dot(segment, permuted, preferred_element_type=jnp.float32)  18.7 us
  transfers between devices with their start and end apart: 24, of which 9 were waited for; matrix products, arithmetic and copies ran while one was open for 24% of the time, Pallas kernels for 0%

profile of v1, /device:TPU:8, one launch (start us, length us, event | category | flops | bytes accessed | tf_op | source)
XLA Modules:
  0.0 500.8 jit_solution(13373064167385995998)
XLA Ops:
  7.2 2.4 fusion.88
  9.8 1.7 collective-permute-start.6
  11.4 0.7 collective-permute-start.8
  12.1 11.4 %collective-permute-done.6 = bf16[512,512]{1,0:T(8,128)(2,1)S(1)} collective-permute-done((bf16[512,512]{1,0:T(8,128)(2,1)S(1)}, bf16[512,512]{1,0:T(8,128)(2,1)S(1)}, u32[]{:S(2)}, u32[]{:S(2)}) %collective-permute-start.6) | collective-permute-done | bytes 524320 | tf_op jit(solution)/shard_map/ppermute | solution.py:13
  23.5 1.6 collective-permute-start.7
  25.1 35.1 %all-gather.1 = bf16[1,1,2048]{2,1,0:T(2,128)(2,1)S(1)} all-gather(bf16[1,1,128]{2,1,0:T(2,128)(2,1)S(1)} %slice.51), channel_id=3, replica_groups=mesh['loop'=16,'row'=4,'col'=4] {'row','col'}, dimensions={2}, use_global_device_ids=true | all-gather | bytes 4352 | tf_op jit(solution)/shard_map/all_gather | solution.py:27
  60.2 13.1 %gather_fusion.5 = bf16[2048]{0:T(1024)(128)(2,1)S(1)} fusion(bf16[2048]{0:T(1024)(128)(2,1)S(1)} %reduce, s32[2048]{0:T(1024)S(1)} %fusion.73), kind=kCustom, calls=%fused_computation.1.clone | custom fusion | bytes 16384 | tf_op jit(solution)/shard_map/jit(_take)/gather | solution.py:29
  73.4 0.8 copy-done.4
  74.2 4.1 fusion.17
  78.3 11.1 %gather_fusion = bf16[2048,512]{1,0:T(8,128)(2,1)} fusion(bf16[2048,512]{1,0:T(8,128)(2,1)} %bitcast.59, s32[2048]{0:T(1024)S(1)} %fusion.73), kind=kCustom, calls=%fused_computation.clone | custom fusion | bytes 4202496 | tf_op jit(solution)/shard_map/jit(_take)/gather | solution.py:28
  89.4 3.7 fusion.50
  93.2 1.8 collective-permute-start.3
  95.0 2.8 collective-permute-start.5
  97.8 7.4 %collective-permute-done.3 = bf16[512,512]{1,0:T(8,128)(2,1)} collective-permute-done((bf16[512,512]{1,0:T(8,128)(2,1)S(1)}, bf16[512,512]{1,0:T(8,128)(2,1)}, u32[]{:S(2)}, u32[]{:S(2)}) %collective-permute-start.3) | collective-permute-done | bytes 524320 | tf_op jit(solution)/shard_map/ppermute | solution.py:13
  105.2 2.0 collective-permute-start.4
  107.2 0.6 fusion.90
  107.9 0.1 fusion.82
  107.9 35.9 %all-gather.2 = bf16[16,1,128]{2,1,0:T(2,128)(2,1)S(1)} all-gather(bf16[1,1,128]{2,1,0:T(2,128)(2,1)S(1)} %fusion.82), channel_id=1, replica_groups=mesh['loop'=16,'row'=4,'col'=4] {'row','col'}, dimensions={0}, use_global_device_ids=true | all-gather | bytes 4352 | tf_op jit(solution)/shard_map/all_gather | solution.py:27
  143.9 13.1 %gather_fusion.6 = bf16[2048]{0:T(1024)(128)(2,1)S(1)} fusion(bf16[2048]{0:T(1024)(128)(2,1)S(1)} %bitcast.56, s32[2048]{0:T(1024)S(1)} %fusion.74), kind=kCustom, calls=%fused_computation.6.clone | custom fusion | bytes 16384 | tf_op jit(solution)/shard_map/jit(_take)/gather | solution.py:29
  157.0 3.9 fusion.24
  161.0 11.1 %gather_fusion.1 = bf16[2048,512]{1,0:T(8,128)(2,1)} fusion(bf16[2048,512]{1,0:T(8,128)(2,1)} %all-gather.12.cloned.1.call-done, s32[2048]{0:T(1024)S(1)} %fusion.74), kind=kCustom, calls=%fused_computation.2.clone | custom fusion | bytes 4202496 | tf_op jit(solution)/shard_map/jit(_take)/gather | solution.py:28
  172.1 3.7 fusion.53
  175.9 2.3 collective-permute-start
  178.2 2.8 collective-permute-start.2
  181.0 7.1 %collective-permute-done = bf16[512,512]{1,0:T(8,128)(2,1)S(1)} collective-permute-done((bf16[512,512]{1,0:T(8,128)(2,1)S(1)}, bf16[512,512]{1,0:T(8,128)(2,1)S(1)}, u32[]{:S(2)}, u32[]{:S(2)}) %collective-permute-start) | collective-permute-done | bytes 524320 | tf_op jit(solution)/shard_map/ppermute | solution.py:13
  188.1 2.2 collective-permute-start.1
  190.3 0.6 fusion.91
  191.0 35.7 %all-gather.3 = bf16[16,1,128]{2,1,0:T(2,128)(2,1)S(1)} all-gather(bf16[1,1,128]{2,1,0:T(2,128)(2,1)S(1)} %fusion.80), channel_id=1, replica_groups=mesh['loop'=16,'row'=4,'col'=4] {'row','col'}, dimensions={0}, use_global_device_ids=true | all-gather | bytes 4352 | tf_op jit(solution)/shard_map/all_gather | solution.py:27
  226.7 13.1 %gather_fusion.7 = bf16[2048]{0:T(1024)(128)(2,1)S(1)} fusion(bf16[2048]{0:T(1024)(128)(2,1)S(1)} %bitcast.57, s32[2048]{0:T(1024)S(1)} %fusion.75), kind=kCustom, calls=%fused_computation.7.clone | custom fusion | bytes 16384 | tf_op jit(solution)/shard_map/jit(_take)/gather | solution.py:29
  239.9 3.8 fusion.31
  243.7 11.1 %gather_fusion.2 = bf16[2048,512]{1,0:T(8,128)(2,1)} fusion(bf16[2048,512]{1,0:T(8,128)(2,1)} %all-gather.14.cloned.1.call-done, s32[2048]{0:T(1024)S(1)} %fusion.75), kind=kCustom, calls=%fused_computation.3.clone | custom fusion | bytes 4202496 | tf_op jit(solution)/shard_map/jit(_take)/gather | solution.py:28
  254.8 3.1 fusion.56
  257.9 0.8 collective-permute-start.12
  258.6 15.0 %collective-permute-done.12 = bf16[512,512]{0,1:T(8,128)(2,1)S(1)} collective-permute-done((bf16[512,512]{0,1:T(8,128)(2,1)S(1)}, bf16[512,512]{0,1:T(8,128)(2,1)S(1)}, u32[]{:S(2)}, u32[]{:S(2)}) %collective-permute-start.12) | collective-permute-done | bytes 524320 | tf_op jit(solution)/shard_map/ppermute | solution.py:22
  273.6 0.8 copy-done.5
  274.5 2.0 collective-permute-start.9
  276.5 0.9 constant_dynamic-slice_fusion
  277.4 0.6 fusion.92
  278.1 0.5 collective-permute-start.11
  278.6 6.8 %collective-permute-done.9 = bf16[512,512]{0,1:T(8,128)(2,1)S(1)} collective-permute-done((bf16[512,512]{0,1:T(8,128)(2,1)S(1)}, bf16[512,512]{0,1:T(8,128)(2,1)S(1)}, u32[]{:S(2)}, u32[]{:S(2)}) %collective-permute-start.9) | collective-permute-done | bytes 524320 | tf_op jit(solution)/shard_map/ppermute | solution.py:13
  285.4 2.7 collective-permute-start.10
  288.2 5.6 %collective-permute-done.17 = bf16[128]{0:T(256)(128)(2,1)S(1)} collective-permute-done((bf16[128]{0:T(256)(128)(2,1)S(1)}, bf16[128]{0:T(256)(128)(2,1)S(1)}, u32[]{:S(2)}, u32[]{:S(2)}) %collective-permute-start.17) | collective-permute-done | bytes 288 | tf_op jit(solution)/shard_map/ppermute | solution.py:22
  293.8 33.9 %all-gather.4 = bf16[16,1,128]{2,1,0:T(2,128)(2,1)S(1)} all-gather(bf16[1,1,128]{2,1,0:T(2,128)(2,1)S(1)} %bitcast.76), channel_id=1, replica_groups=mesh['loop'=16,'row'=4,'col'=4] {'row','col'}, dimensions={0}, use_global_device_ids=true | all-gather | bytes 4352 | tf_op jit(solution)/shard_map/all_gather | solution.py:27
  327.7 13.1 %gather_fusion.8 = bf16[2048]{0:T(1024)(128)(2,1)S(1)} fusion(bf16[2048]{0:T(1024)(128)(2,1)S(1)} %bitcast.58, s32[2048]{0:T(1024)S(1)} %fusion.76), kind=kCustom, calls=%fused_computation.8.clone | custom fusion | bytes 16384 | tf_op jit(solution)/shard_map/jit(_take)/gather | solution.py:29
  340.9 20.3 %fusion.10 = bf16[512,2048]{0,1:T(8,128)(2,1)} fusion(s32[]{:T(128)S(6)} %select_n.72, bf16[512,512]{0,1:T(8,128)(2,1)S(1)} %collective-permute-done.10, bf16[512,512]{0,1:T(8,128)(2,1)S(1)} %collective-permute-done.9, bf16[512,512]{0,1:T(8,128)(2,1)S(1)} %fusion.56, bf16[512,512]{0,1:T(8,128)(2,1)S(1)} %collective-permute-done.11), kind=kLoop, calls=%fused_computation.60 | loop fusion | flops 16777216 | bytes 4194308 | tf_op jit(solution)/shard_map/jit(_roll_dynamic)/concatenate | solution.py:17
  361.2 2.9 copy.10
  364.0 9.3 %gather_fusion.3 = bf16[2048,512]{1,0:T(8,128)(2,1)} fusion(bf16[2048,512]{1,0:T(8,128)(2,1)S(1)} %copy.10, s32[2048]{0:T(1024)S(1)} %fusion.76), kind=kCustom, calls=%fused_computation.4.clone | custom fusion | bytes 4202496 | tf_op jit(solution)/shard_map/jit(_take)/gather | solution.py:28
  373.4 3.9 fusion.59
  377.4 10.4 %collective-permute-done.16 = bf16[512,512]{0,1:T(8,128)(2,1)S(1)} collective-permute-done((bf16[512,512]{0,1:T(8,128)(2,1)S(1)}, bf16[512,512]{0,1:T(8,128)(2,1)S(1)}, u32[]{:S(2)}, u32[]{:S(2)}) %collective-permute-start.16) | collective-permute-done | bytes 524320 | tf_op jit(solution)/shard_map/ppermute | solution.py:22
  387.7 0.8 copy-done.6
  388.5 3.6 collective-permute-start.13
  392.2 0.4 fusion.93
  392.5 8.2 %collective-permute-done.13 = bf16[512,512]{0,1:T(8,128)(2,1)S(1)} collective-permute-done((bf16[512,512]{0,1:T(8,128)(2,1)S(1)}, bf16[512,512]{0,1:T(8,128)(2,1)S(1)}, u32[]{:S(2)}, u32[]{:S(2)}) %collective-permute-start.13) | collective-permute-done | bytes 524320 | tf_op jit(solution)/shard_map/ppermute | solution.py:13
  400.8 3.9 collective-permute-start.14
  404.8 4.7 collective-permute-done.18
  409.5 33.5 %all-gather.5 = bf16[16,1,128]{2,1,0:T(2,128)(2,1)S(1)} all-gather(bf16[1,1,128]{2,1,0:T(2,128)(2,1)S(1)} %bitcast.75), channel_id=1, replica_groups=mesh['loop'=16,'row'=4,'col'=4] {'row','col'}, dimensions={0}, use_global_device_ids=true | all-gather | bytes 4352 | tf_op jit(solution)/shard_map/all_gather | solution.py:27
  443.0 13.1 %gather_fusion.9 = bf16[2048]{0:T(1024)(128)(2,1)S(1)} fusion(bf16[2048]{0:T(1024)(128)(2,1)S(1)} %bitcast.55, s32[2048]{0:T(1024)S(1)} %fusion.77), kind=kCustom, calls=%fused_computation.9.clone | custom fusion | bytes 16384 | tf_op jit(solution)/shard_map/jit(_take)/gather | solution.py:29
  456.2 19.1 %fusion.3 = bf16[512,2048]{0,1:T(8,128)(2,1)S(1)} fusion(s32[]{:T(128)S(6)} %select_n.72, bf16[512,512]{0,1:T(8,128)(2,1)S(1)} %collective-permute-done.14, bf16[512,512]{0,1:T(8,128)(2,1)S(1)} %collective-permute-done.13, bf16[512,512]{0,1:T(8,128)(2,1)S(1)} %fusion.59, bf16[512,512]{0,1:T(8,128)(2,1)S(1)} %collective-permute-done.15), kind=kLoop, calls=%fused_computation.53 | loop fusion | flops 16777216 | bytes 4194308 | tf_op jit(solution)/shard_map/jit(_roll_dynamic)/concatenate | solution.py:17
  475.3 1.3 copy-done.1
  476.7 0.4 fusion.94
  477.0 0.6 add_bitcast_fusion
  477.7 2.9 copy.11
  480.5 9.2 %gather_fusion.4 = bf16[2048,512]{1,0:T(8,128)(2,1)} fusion(bf16[2048,512]{1,0:T(8,128)(2,1)S(1)} %copy.11, s32[2048]{0:T(1024)S(1)} %fusion.77), kind=kCustom, calls=%fused_computation.5.clone | custom fusion | bytes 4202496 | tf_op jit(solution)/shard_map/jit(_take)/gather | solution.py:28
  489.7 4.3 fusion.65
  (68 shorter events, 1.0 us)
Async XLA Ops:
  7.2 17.9 %copy-start.7 = (s32[1,3,2048]{2,0,1:T(1,128)S(1)}, s32[1,3,2048]{2,0,1:T(1,128)}, u32[]{:S(2)}) copy-start(s32[1,3,2048]{2,0,1:T(1,128)} %param.11) | copy-start | bytes 73732
  7.2 17.9 %copy-start.8 = (bf16[1,4,128]{2,1,0:T(4,128)(2,1)S(1)}, bf16[1,4,128]{2,1,0:T(4,128)(2,1)}, u32[]{:S(2)}) copy-start(bf16[1,4,128]{2,1,0:T(4,128)(2,1)} %param.13) | copy-start | bytes 3076
  7.2 71.1 %all-gather.20.cloned.1.call-start = ((), (), s32[]{:S(2)}) async-start(), calls=%async_computation.4 | async-start | bytes 2621440 | tf_op jit(solution)/shard_map/all_gather | solution.py:26
  9.7 63.6 %copy-start.2 = (bf16[512,512]{1,0:T(8,128)(2,1)}, bf16[512,512]{1,0:T(8,128)(2,1)S(1)}, u32[]{:S(2)}) copy-start(bf16[512,512]{1,0:T(8,128)(2,1)S(1)} %get-tuple-element.18) | copy-start | bytes 1572868
  9.7 151.3 %all-gather.12.cloned.1.call-start = ((), (), s32[]{:S(2)}) async-start(), calls=%async_computation | async-start | bytes 2621440 | tf_op jit(solution)/shard_map/all_gather | solution.py:26
  9.8 13.7 %collective-permute-start.6 = (bf16[512,512]{1,0:T(8,128)(2,1)S(1)}, bf16[512,512]{1,0:T(8,128)(2,1)S(1)}, u32[]{:S(2)}, u32[]{:S(2)}) collective-permute-start(bf16[512,512]{1,0:T(8,128)(2,1)S(1)} %get-tuple-element.18), channel_id=1, source_target_pairs={{0,1},{1,2},{2,3},{3,0},{4,5},{5,6},{6,7},{7,4},{8,9},{9,10},{10,1... | collective-permute-start | bytes 1572872 | tf_op jit(solution)/shard_map/ppermute | solution.py:13
  11.4 61.9 %collective-permute-start.8 = (bf16[512,512]{1,0:T(8,128)(2,1)S(1)}, bf16[512,512]{1,0:T(8,128)(2,1)S(1)}, u32[]{:S(2)}, u32[]{:S(2)}) collective-permute-start(bf16[512,512]{1,0:T(8,128)(2,1)S(1)} %get-tuple-element.18), channel_id=1, source_target_pairs={{0,3},{1,0},{2,1},{3,2},{4,7},{5,4},{6,5},{7,6},{8,11},{9,8},{10,9... | collective-permute-start | bytes 1572872 | tf_op jit(solution)/shard_map/ppermute | solution.py:15
  23.5 49.8 %copy-start.3 = (bf16[512,512]{1,0:T(8,128)(2,1)}, bf16[512,512]{1,0:T(8,128)(2,1)S(1)}, u32[]{:S(2)}) copy-start(bf16[512,512]{1,0:T(8,128)(2,1)S(1)} %collective-permute-done.6) | copy-start | bytes 1572868
  23.5 50.7 %collective-permute-start.7 = (bf16[512,512]{1,0:T(8,128)(2,1)S(1)}, bf16[512,512]{1,0:T(8,128)(2,1)}, u32[]{:S(2)}, u32[]{:S(2)}) collective-permute-start(bf16[512,512]{1,0:T(8,128)(2,1)S(1)} %collective-permute-done.6), channel_id=1, source_target_pairs={{0,1},{1,2},{2,3},{3,0},{4,5},{5,6},{6,7},{7,4},{8,9},{9,10},{10,1... | collective-permute-start | bytes 1572872 | tf_op jit(solution)/shard_map/ppermute | solution.py:13
  73.3 0.8 copy-start.4
  93.2 150.5 %all-gather.14.cloned.1.call-start = ((), (), s32[]{:S(2)}) async-start(), calls=%async_computation.1 | async-start | bytes 2621440 | tf_op jit(solution)/shard_map/all_gather | solution.py:26
  93.2 12.0 %collective-permute-start.3 = (bf16[512,512]{1,0:T(8,128)(2,1)S(1)}, bf16[512,512]{1,0:T(8,128)(2,1)}, u32[]{:S(2)}, u32[]{:S(2)}) collective-permute-start(bf16[512,512]{1,0:T(8,128)(2,1)S(1)} %get-tuple-element.16), channel_id=1, source_target_pairs={{0,1},{1,2},{2,3},{3,0},{4,5},{5,6},{6,7},{7,4},{8,9},{9,10},{10,1... | collective-permute-start | bytes 1572872 | tf_op jit(solution)/shard_map/ppermute | solution.py:13
  95.0 62.0 %collective-permute-start.5 = (bf16[512,512]{1,0:T(8,128)(2,1)S(1)}, bf16[512,512]{1,0:T(8,128)(2,1)}, u32[]{:S(2)}, u32[]{:S(2)}) collective-permute-start(bf16[512,512]{1,0:T(8,128)(2,1)S(1)} %get-tuple-element.16), channel_id=1, source_target_pairs={{0,3},{1,0},{2,1},{3,2},{4,7},{5,4},{6,5},{7,6},{8,11},{9,8},{10,9... | collective-permute-start | bytes 1572872 | tf_op jit(solution)/shard_map/ppermute | solution.py:15
  105.2 51.8 %collective-permute-start.4 = (bf16[512,512]{1,0:T(8,128)(2,1)}, bf16[512,512]{1,0:T(8,128)(2,1)}, u32[]{:S(2)}, u32[]{:S(2)}) collective-permute-start(bf16[512,512]{1,0:T(8,128)(2,1)} %collective-permute-done.3), channel_id=1, source_target_pairs={{0,1},{1,2},{2,3},{3,0},{4,5},{5,6},{6,7},{7,4},{8,9},{9,10},{10,1... | collective-permute-start | bytes 1572872 | tf_op jit(solution)/shard_map/ppermute | solution.py:13
  175.8 185.3 %all-gather.16.cloned.1.call-start = ((), (), s32[]{:S(2)}) async-start(), calls=%async_computation.2 | async-start | bytes 2621440 | tf_op jit(solution)/shard_map/all_gather | solution.py:26
  175.9 12.2 %collective-permute-start = (bf16[512,512]{1,0:T(8,128)(2,1)S(1)}, bf16[512,512]{1,0:T(8,128)(2,1)S(1)}, u32[]{:S(2)}, u32[]{:S(2)}) collective-permute-start(bf16[512,512]{1,0:T(8,128)(2,1)S(1)} %get-tuple-element.17), channel_id=1, source_target_pairs={{0,1},{1,2},{2,3},{3,0},{4,5},{5,6},{6,7},{7,4},{8,9},{9,10},{10,1... | collective-permute-start | bytes 1572872 | tf_op jit(solution)/shard_map/ppermute | solution.py:13
  178.2 61.7 %collective-permute-start.2 = (bf16[512,512]{1,0:T(8,128)(2,1)S(1)}, bf16[512,512]{1,0:T(8,128)(2,1)}, u32[]{:S(2)}, u32[]{:S(2)}) collective-permute-start(bf16[512,512]{1,0:T(8,128)(2,1)S(1)} %get-tuple-element.17), channel_id=1, source_target_pairs={{0,3},{1,0},{2,1},{3,2},{4,7},{5,4},{6,5},{7,6},{8,11},{9,8},{10,9... | collective-permute-start | bytes 1572872 | tf_op jit(solution)/shard_map/ppermute | solution.py:15
  188.1 51.8 %collective-permute-start.1 = (bf16[512,512]{1,0:T(8,128)(2,1)S(1)}, bf16[512,512]{1,0:T(8,128)(2,1)}, u32[]{:S(2)}, u32[]{:S(2)}) collective-permute-start(bf16[512,512]{1,0:T(8,128)(2,1)S(1)} %collective-permute-done), channel_id=1, source_target_pairs={{0,1},{1,2},{2,3},{3,0},{4,5},{5,6},{6,7},{7,4},{8,9},{9,10},{10,1... | collective-permute-start | bytes 1572872 | tf_op jit(solution)/shard_map/ppermute | solution.py:13
  257.9 15.7 %collective-permute-start.12 = (bf16[512,512]{0,1:T(8,128)(2,1)S(1)}, bf16[512,512]{0,1:T(8,128)(2,1)S(1)}, u32[]{:S(2)}, u32[]{:S(2)}) collective-permute-start(bf16[512,512]{0,1:T(8,128)(2,1)S(1)} %fusion.56), channel_id=1, source_target_pairs={{0,16},{16,32},{32,48},{48,64},{64,80},{80,96},{96,112},{112,128},... | collective-permute-start | bytes 1572872 | tf_op jit(solution)/shard_map/ppermute | solution.py:22
  273.6 0.8 copy-start.5
  274.4 203.2 %all-gather.18.cloned.1.call-start = ((), (), s32[]{:S(2)}) async-start(), calls=%async_computation.3 | async-start | bytes 2621440 | tf_op jit(solution)/shard_map/all_gather | solution.py:26
  274.5 10.9 %collective-permute-start.9 = (bf16[512,512]{0,1:T(8,128)(2,1)S(1)}, bf16[512,512]{0,1:T(8,128)(2,1)S(1)}, u32[]{:S(2)}, u32[]{:S(2)}) collective-permute-start(bf16[512,512]{0,1:T(8,128)(2,1)S(1)} %fusion.56), channel_id=1, source_target_pairs={{0,1},{1,2},{2,3},{3,0},{4,5},{5,6},{6,7},{7,4},{8,9},{9,10},{10,1... | collective-permute-start | bytes 1572872 | tf_op jit(solution)/shard_map/ppermute | solution.py:13
  278.1 62.8 %collective-permute-start.11 = (bf16[512,512]{0,1:T(8,128)(2,1)S(1)}, bf16[512,512]{0,1:T(8,128)(2,1)S(1)}, u32[]{:S(2)}, u32[]{:S(2)}) collective-permute-start(bf16[512,512]{0,1:T(8,128)(2,1)S(1)} %fusion.56), channel_id=1, source_target_pairs={{0,3},{1,0},{2,1},{3,2},{4,7},{5,4},{6,5},{7,6},{8,11},{9,8},{10,9... | collective-permute-start | bytes 1572872 | tf_op jit(solution)/shard_map/ppermute | solution.py:15
  285.4 55.5 %collective-permute-start.10 = (bf16[512,512]{0,1:T(8,128)(2,1)S(1)}, bf16[512,512]{0,1:T(8,128)(2,1)S(1)}, u32[]{:S(2)}, u32[]{:S(2)}) collective-permute-start(bf16[512,512]{0,1:T(8,128)(2,1)S(1)} %collective-permute-done.9), channel_id=1, source_target_pairs={{0,1},{1,2},{2,3},{3,0},{4,5},{5,6},{6,7},{7,4},{8,9},{9,10},{10,1... | collective-permute-start | bytes 1572872 | tf_op jit(solution)/shard_map/ppermute | solution.py:13
  288.1 5.7 %collective-permute-start.17 = (bf16[128]{0:T(256)(128)(2,1)S(1)}, bf16[128]{0:T(256)(128)(2,1)S(1)}, u32[]{:S(2)}, u32[]{:S(2)}) collective-permute-start(bf16[128]{0:T(256)(128)(2,1)S(1)} %fusion.78), channel_id=1, source_target_pairs={{0,16},{16,32},{32,48},{48,64},{64,80},{80,96},{96,112},{112,128},... | collective-permute-start | bytes 776 | tf_op jit(solution)/shard_map/ppermute | solution.py:22
  373.4 18.8 %copy-start = (bf16[512,2048]{0,1:T(8,128)(2,1)S(1)}, bf16[512,2048]{0,1:T(8,128)(2,1)}, u32[]{:S(2)}) copy-start(bf16[512,2048]{0,1:T(8,128)(2,1)} %fusion.10) | copy-start | bytes 6291460
  377.3 10.5 %collective-permute-start.16 = (bf16[512,512]{0,1:T(8,128)(2,1)S(1)}, bf16[512,512]{0,1:T(8,128)(2,1)S(1)}, u32[]{:S(2)}, u32[]{:S(2)}) collective-permute-start(bf16[512,512]{0,1:T(8,128)(2,1)S(1)} %fusion.59), channel_id=1, source_target_pairs={{0,32},{16,48},{32,64},{48,80},{64,96},{80,112},{96,128},{112,144}... | collective-permute-start | bytes 1572872 | tf_op jit(solution)/shard_map/ppermute | solution.py:22
  387.7 0.8 copy-start.6
  388.5 12.2 %collective-permute-start.13 = (bf16[512,512]{0,1:T(8,128)(2,1)S(1)}, bf16[512,512]{0,1:T(8,128)(2,1)S(1)}, u32[]{:S(2)}, u32[]{:S(2)}) collective-permute-start(bf16[512,512]{0,1:T(8,128)(2,1)S(1)} %fusion.59), channel_id=1, source_target_pairs={{0,1},{1,2},{2,3},{3,0},{4,5},{5,6},{6,7},{7,4},{8,9},{9,10},{10,1... | collective-permute-start | bytes 1572872 | tf_op jit(solution)/shard_map/ppermute | solution.py:13
  392.5 63.6 %collective-permute-start.15 = (bf16[512,512]{0,1:T(8,128)(2,1)S(1)}, bf16[512,512]{0,1:T(8,128)(2,1)S(1)}, u32[]{:S(2)}, u32[]{:S(2)}) collective-permute-start(bf16[512,512]{0,1:T(8,128)(2,1)S(1)} %fusion.59), channel_id=1, source_target_pairs={{0,3},{1,0},{2,1},{3,2},{4,7},{5,4},{6,5},{7,6},{8,11},{9,8},{10,9... | collective-permute-start | bytes 1572872 | tf_op jit(solution)/shard_map/ppermute | solution.py:15
  400.8 55.4 %collective-permute-start.14 = (bf16[512,512]{0,1:T(8,128)(2,1)S(1)}, bf16[512,512]{0,1:T(8,128)(2,1)S(1)}, u32[]{:S(2)}, u32[]{:S(2)}) collective-permute-start(bf16[512,512]{0,1:T(8,128)(2,1)S(1)} %collective-permute-done.13), channel_id=1, source_target_pairs={{0,1},{1,2},{2,3},{3,0},{4,5},{5,6},{6,7},{7,4},{8,9},{9,10},{10,1... | collective-permute-start | bytes 1572872 | tf_op jit(solution)/shard_map/ppermute | solution.py:13
  404.8 4.8 collective-permute-start.18
  475.3 1.3 copy-start.1
Sparse Core Ops, SparseCore 0:
  10.4 32.0 all-gather.19
  93.3 32.1 all-gather.11
  175.9 32.9 all-gather.13
  274.6 29.4 all-gather.15
  388.7 31.8 all-gather.17
